TPU v7x, 32 devices: a whole 2x2x4 slice. The times are simulated.
32 devices in a mesh: replica: 8 (over y, x, core), tensor: 4 (over z).
Axes of the slice: x: 2, y: 2, z: 4, core: 2. Of those that a mesh axis runs over, the one named last changes fastest.
Arguments:
- weight: bfloat16 [8, 4096, 2048], P('replica', None, 'tensor'), may hold values from -0.09375 to 0.09375
- momentum: bfloat16 [8, 4096, 2048], P('replica', None, 'tensor'), may hold values from -24 to 24
- inputs: bfloat16 [2, 4096, 4096], P(None, ('replica', 'tensor')), may hold values from -6 to 6
- out_grads: bfloat16 [2, 4096, 2048], P(None, 'replica', 'tensor'), may hold values from -6 to 6
Outputs:
- new_weight: bfloat16 [8, 4096, 2048], P('replica', None, 'tensor')
- new_momentum: bfloat16 [8, 4096, 2048], P('replica', None, 'tensor')
- input_grad: bfloat16 [2, 4096, 4096], P(None, ('replica', 'tensor'))
All inputs are finite; a program needn't handle non-finite values.
Results may differ from a plain program's by a relative error of at most 0.014.
Values may be sent and summed in bfloat16 or wider, within the bound.
No kernel may reach another device: no remote copies, remote signals or barrier semaphores. Data moves between devices by JAX's collectives and lax.ppermute only.
A program may use at most 128 MiB of HBM per device.

v0:
```python
import jax
import jax.numpy as jnp
from jax import lax
from jax.sharding import PartitionSpec as P

learn_rate = 0.001
mom_decay = 0.9


def from_partner(block, axis, distance):
    count = lax.axis_size(axis)
    route = []
    for low in range(count):
        high = low | 1 << distance
        if high != low and high < count:
            route += [(low, high), (high, low)]
    return lax.ppermute(block, axis, route)


def silu_slope(pre):
    sigma = jax.nn.sigmoid(pre)
    return sigma * (1.0 + pre * (1.0 - sigma))


def input_partials(slope_grad, weight_now):
    partial_value = lax.dot_general(
        slope_grad, weight_now, (((1,), (1,)), ((), ())), preferred_element_type=jnp.float32
    )
    rounded = partial_value.astype(jnp.bfloat16)
    return (
        lax.psum_scatter(rounded, "tensor", scatter_dimension=0, tiled=True)
        .astype(jnp.float32)
        .astype(jnp.bfloat16)
    )


def gossip_update(weight_now, moment_now, grad_w, step):
    moment_new = (mom_decay * moment_now.astype(jnp.float32) + grad_w).astype(jnp.bfloat16)
    stepped = (weight_now.astype(jnp.float32) - learn_rate * moment_new.astype(jnp.float32)).astype(
        jnp.bfloat16
    )
    other_weight, other_moment = from_partner((stepped, moment_new), "replica", step)
    averaged = ((stepped.astype(jnp.float32) + other_weight.astype(jnp.float32)) * 0.5).astype(
        jnp.bfloat16
    )
    moment_avg = ((moment_new.astype(jnp.float32) + other_moment.astype(jnp.float32)) * 0.5).astype(
        jnp.bfloat16
    )
    return (averaged, moment_avg)


def local(weight, momentum, inputs, out_grads):
    weight_now = weight[0]
    moment_now = momentum[0]
    grads_out = []
    for step in range(inputs.shape[0]):
        rows_here = inputs[step]
        gathered = lax.all_gather(rows_here, "tensor", axis=0, tiled=True)
        pre = jnp.dot(gathered, weight_now, preferred_element_type=jnp.float32)
        slope_grad = (out_grads[step].astype(jnp.float32) * silu_slope(pre)).astype(jnp.bfloat16)
        grad_w = lax.dot_general(
            gathered, slope_grad, (((0,), (0,)), ((), ())), preferred_element_type=jnp.float32
        )
        grads_out.append(input_partials(slope_grad, weight_now))
        next_weight, next_moment = gossip_update(weight_now, moment_now, grad_w, step)
        weight_now = next_weight
        moment_now = next_moment
    return (weight_now[None], moment_now[None], jnp.stack(grads_out))


def solution(mesh):
    return jax.shard_map(
        local,
        mesh=mesh,
        in_specs=(
            P("replica", None, "tensor"),
            P("replica", None, "tensor"),
            P(None, ("replica", "tensor"), None),
            P(None, "replica", "tensor"),
        ),
        out_specs=(
            P("replica", None, "tensor"),
            P("replica", None, "tensor"),
            P(None, ("replica", "tensor"), None),
        ),
        check_vma=False,
    )
```

profile of v0, /device:TPU:0, one launch (start us, length us, event | category | flops | bytes accessed | tf_op | source)
XLA Modules:
  0.0 406.5 jit_solution(11764880076407524908)
XLA Ops:
  7.2 3.1 fusion.48
  10.4 0.7 all-gather.7.cloned.1.call-update
  11.1 82.8 %all-gather.5.cloned.1.call-done = bf16[1,512,4096]{2,1,0:T(8,128)(2,1)} async-done(((bf16[1,128,4096]{2,1,0:T(8,128)(2,1)}), bf16[1,512,4096]{2,1,0:T(8,128)(2,1)}) %all-gather.5.cloned.1.call-update) | async-done | bytes 4194320 | tf_op jit(solution)/shard_map/all_gather | solution.py:58
  93.9 5.9 %fusion.13 = f32[512,512]{1,0:T(8,128)S(1)} fusion(bf16[1,4096,512]{2,1,0:T(8,128)(2,1)} %param.4, bf16[1,512,4096]{2,1,0:T(8,128)(2,1)} %all-gather.5.cloned.1.call-done), kind=kOutput, calls=%fused_computation.23 | convolution fusion | flops 2147483648 | bytes 9437184 | tf_op jit(solution)/shard_map/dot_general | solution.py:59
  99.9 4.5 %convolution_convert_fusion.1 = bf16[512,4096]{1,0:T(8,128)(2,1)} fusion(bf16[1,4096,512]{2,1,0:T(8,128)(2,1)S(1)} %copy-done, f32[512,512]{1,0:T(8,128)S(1)} %fusion.13, bf16[2,512,512]{2,1,0:T(8,128)(2,1)S(1)} %copy-done.2), kind=kOutput, calls=%fused_computation.19 | convolution fusion | flops 2152202240 | bytes 9961472 | tf_op jit(solution)/shard_map/dot_general | solution.py:26
  104.4 0.2 reduce-scatter.5.cloned.1.call-start
  104.7 6.3 %copy.7 = bf16[1,4096,512]{1,2,0:T(8,128)(2,1)} copy(bf16[1,4096,512]{2,1,0:T(8,128)(2,1)} %param.4) | data formatting | bytes 8388608 | tf_op args[0]
  111.0 6.3 %copy.8 = bf16[1,4096,512]{1,2,0:T(8,128)(2,1)} copy(bf16[1,4096,512]{2,1,0:T(8,128)(2,1)} %param.5) | data formatting | bytes 8388608 | tf_op args[1]
  117.3 9.6 %fusion.1 = (bf16[4096,512]{0,1:T(8,128)(2,1)}, bf16[4096,512]{0,1:T(8,128)(2,1)}) fusion(bf16[1,4096,512]{1,2,0:T(8,128)(2,1)} %copy.7, bf16[1,512,4096]{2,1,0:T(8,128)(2,1)} %all-gather.5.cloned.1.call-done, f32[512,512]{1,0:T(8,128)S(1)} %fusion.13, bf16[2,512,512]{2,1,0:T(8,128)(2,1)S(1)} %copy-done.2, bf16[1,4096,512]{1,2,0:T(8,128)(2,1)} %copy.8), kind=kOutput, calls=%fused_computation.5 | convolution fusion | flops 2168979456 | bytes 22544384 | tf_op jit(solution)/shard_map/dot_general | solution.py:61
  127.0 0.5 collective-permute-start.1
  127.5 47.9 %all-gather.7.cloned.1.call-done = bf16[1,512,4096]{2,1,0:T(8,128)(2,1)} async-done(((bf16[1,128,4096]{2,1,0:T(8,128)(2,1)}), bf16[1,512,4096]{2,1,0:T(8,128)(2,1)}) %all-gather.7.cloned.1.call-update) | async-done | bytes 4194320 | tf_op jit(solution)/shard_map/all_gather | solution.py:58
  175.3 7.2 %fusion.23 = f32[512,512]{1,0:T(8,128)S(1)} fusion(bf16[1,512,4096]{2,1,0:T(8,128)(2,1)} %all-gather.7.cloned.1.call-done, bf16[4096,512]{0,1:T(8,128)(2,1)} %collective-permute-done, bf16[4096,512]{0,1:T(8,128)(2,1)} %get-tuple-element.10), kind=kOutput, calls=%fused_computation.32 | convolution fusion | flops 2157969408 | bytes 13631488 | tf_op jit(solution)/shard_map/dot_general | solution.py:59
  182.5 9.3 %fusion.8 = bf16[4096,512]{0,1:T(8,128)(2,1)} fusion(bf16[4096,512]{0,1:T(8,128)(2,1)} %collective-permute-done.1, bf16[4096,512]{0,1:T(8,128)(2,1)} %get-tuple-element.11, bf16[1,512,4096]{2,1,0:T(8,128)(2,1)S(1)} %copy-done.1, f32[512,512]{1,0:T(8,128)S(1)} %fusion.23, bf16[2,512,512]{2,1,0:T(8,128)(2,1)S(1)} %copy-done.2), kind=kOutput, calls=%fused_computation.13 | convolution fusion | flops 2168979456 | bytes 18350080 | tf_op jit(solution)/shard_map/dot_general | solution.py:61
  191.8 1.7 collective-permute-start.3
  193.5 8.1 %convolution_convert_fusion = bf16[512,4096]{1,0:T(8,128)(2,1)} fusion(f32[512,512]{1,0:T(8,128)S(1)} %fusion.23, bf16[2,512,512]{2,1,0:T(8,128)(2,1)S(1)} %copy-done.2, bf16[4096,512]{0,1:T(8,128)(2,1)} %collective-permute-done, bf16[4096,512]{0,1:T(8,128)(2,1)} %get-tuple-element.10), kind=kOutput, calls=%fused_computation.18 | convolution fusion | flops 2162688000 | bytes 14155776 | tf_op jit(solution)/shard_map/dot_general | solution.py:26
  201.7 82.9 %collective-permute-done.3 = bf16[4096,512]{0,1:T(8,128)(2,1)} collective-permute-done((bf16[4096,512]{0,1:T(8,128)(2,1)}, bf16[4096,512]{0,1:T(8,128)(2,1)}, u32[]{:S(2)}, u32[]{:S(2)}) %collective-permute-start.3) | collective-permute-done | bytes 4194336 | tf_op jit(solution)/shard_map/ppermute | solution.py:17
  284.6 9.9 %fusion.11 = (bf16[1,4096,512]{1,2,0:T(8,128)(2,1)}, bf16[4096,512]{0,1:T(8,128)(2,1)}) fusion(bf16[4096,512]{0,1:T(8,128)(2,1)} %collective-permute-done.3, bf16[4096,512]{0,1:T(8,128)(2,1)} %fusion.8, bf16[4096,512]{0,1:T(8,128)(2,1)} %collective-permute-done, bf16[4096,512]{0,1:T(8,128)(2,1)} %get-tuple-element.10), kind=kLoop, calls=%fused_computation.21 | loop fusion | flops 29360128 | bytes 25165824 | tf_op jit(solution)/shard_map/broadcast_in_dim | solution.py:68
  294.5 1.6 collective-permute-start.2
  296.0 6.4 %copy.11 = bf16[1,4096,512]{2,1,0:T(8,128)(2,1)} copy(bf16[1,4096,512]{1,2,0:T(8,128)(2,1)} %get-tuple-element.6) | data formatting | bytes 8388608
  302.5 30.0 %reduce-scatter.5.cloned.1.call-done = bf16[128,4096]{1,0:T(8,128)(2,1)} async-done(((bf16[512,4096]{1,0:T(8,128)(2,1)}), bf16[128,4096]{1,0:T(8,128)(2,1)}) %reduce-scatter.5.cloned.1.call-update) | async-done | bytes 1048592 | tf_op jit(solution)/shard_map/reduce_scatter | solution.py:31
  332.4 3.1 pad_maximum_fusion
  335.5 50.9 %collective-permute-done.2 = bf16[4096,512]{0,1:T(8,128)(2,1)} collective-permute-done((bf16[4096,512]{0,1:T(8,128)(2,1)}, bf16[4096,512]{0,1:T(8,128)(2,1)}, u32[]{:S(2)}, u32[]{:S(2)}) %collective-permute-start.2) | collective-permute-done | bytes 4194336 | tf_op jit(solution)/shard_map/ppermute | solution.py:17
  386.4 7.2 %fusion.10 = bf16[1,4096,512]{1,2,0:T(8,128)(2,1)} fusion(bf16[4096,512]{0,1:T(8,128)(2,1)} %collective-permute-done.2, bf16[4096,512]{0,1:T(8,128)(2,1)} %get-tuple-element.7), kind=kLoop, calls=%fused_computation.20 | loop fusion | flops 10485760 | bytes 12582912 | tf_op jit(solution)/shard_map/broadcast_in_dim | solution.py:68
  393.6 6.4 %copy.10 = bf16[1,4096,512]{2,1,0:T(8,128)(2,1)} copy(bf16[1,4096,512]{1,2,0:T(8,128)(2,1)} %fusion.10) | data formatting | bytes 8388608
  (16 shorter events, 0.2 us)
Async XLA Ops:
  7.2 86.8 %all-gather.5.cloned.1.call-start = ((), (), s32[]{:S(2)}) async-start(), calls=%async_computation.4 | async-start | bytes 5242880 | tf_op jit(solution)/shard_map/all_gather | solution.py:58
  10.3 165.0 %all-gather.7.cloned.1.call-start = ((), (), s32[]{:S(2)}) async-start(), calls=%async_computation.5 | async-start | bytes 5242880 | tf_op jit(solution)/shard_map/all_gather | solution.py:58
  11.1 88.8 %copy-start.2 = (bf16[2,512,512]{2,1,0:T(8,128)(2,1)S(1)}, bf16[2,512,512]{2,1,0:T(8,128)(2,1)}, u32[]{:S(2)}) copy-start(bf16[2,512,512]{2,1,0:T(8,128)(2,1)} %param.7) | copy-start | bytes 3145732
  11.1 291.4 %reduce-scatter.3.cloned.1.call-start = ((), (), s32[]{:S(2)}) async-start(), calls=%async_computation.2 | async-start | bytes 5242880 | tf_op jit(solution)/shard_map/reduce_scatter | solution.py:31
  93.9 5.9 %copy-start = (bf16[1,4096,512]{2,1,0:T(8,128)(2,1)S(1)}, bf16[1,4096,512]{2,1,0:T(8,128)(2,1)}, u32[]{:S(2)}) copy-start(bf16[1,4096,512]{2,1,0:T(8,128)(2,1)} %param.4) | copy-start | bytes 12582916
  104.4 228.0 %reduce-scatter.5.cloned.1.call-start = ((), (), s32[]{:S(2)}) async-start(), calls=%async_computation.3 | async-start | bytes 5242880 | tf_op jit(solution)/shard_map/reduce_scatter | solution.py:31
  127.0 48.4 %collective-permute-start = (bf16[4096,512]{0,1:T(8,128)(2,1)}, bf16[4096,512]{0,1:T(8,128)(2,1)}, u32[]{:S(2)}, u32[]{:S(2)}) collective-permute-start(bf16[4096,512]{0,1:T(8,128)(2,1)} %get-tuple-element.10), channel_id=1, source_target_pairs={{0,4},{4,0},{8,12},{12,8},{16,20},{20,16},{24,28},{28,24},{1,5},{5... | collective-permute-start | bytes 12582920 | tf_op jit(solution)/shard_map/ppermute | solution.py:17
  127.0 55.6 %collective-permute-start.1 = (bf16[4096,512]{0,1:T(8,128)(2,1)}, bf16[4096,512]{0,1:T(8,128)(2,1)}, u32[]{:S(2)}, u32[]{:S(2)}) collective-permute-start(bf16[4096,512]{0,1:T(8,128)(2,1)} %get-tuple-element.11), channel_id=1, source_target_pairs={{0,4},{4,0},{8,12},{12,8},{16,20},{20,16},{24,28},{28,24},{1,5},{5... | collective-permute-start | bytes 12582920 | tf_op jit(solution)/shard_map/ppermute | solution.py:17
  175.3 7.2 %copy-start.1 = (bf16[1,512,4096]{2,1,0:T(8,128)(2,1)S(1)}, bf16[1,512,4096]{2,1,0:T(8,128)(2,1)}, u32[]{:S(2)}) copy-start(bf16[1,512,4096]{2,1,0:T(8,128)(2,1)} %all-gather.7.cloned.1.call-done) | copy-start | bytes 12582916
  191.8 92.8 %collective-permute-start.3 = (bf16[4096,512]{0,1:T(8,128)(2,1)}, bf16[4096,512]{0,1:T(8,128)(2,1)}, u32[]{:S(2)}, u32[]{:S(2)}) collective-permute-start(bf16[4096,512]{0,1:T(8,128)(2,1)} %fusion.8), channel_id=1, source_target_pairs={{0,8},{8,0},{4,12},{12,4},{16,24},{24,16},{20,28},{28,20},{1,9},{9... | collective-permute-start | bytes 12582920 | tf_op jit(solution)/shard_map/ppermute | solution.py:17
  294.5 91.9 %collective-permute-start.2 = (bf16[4096,512]{0,1:T(8,128)(2,1)}, bf16[4096,512]{0,1:T(8,128)(2,1)}, u32[]{:S(2)}, u32[]{:S(2)}) collective-permute-start(bf16[4096,512]{0,1:T(8,128)(2,1)} %get-tuple-element.7), channel_id=1, source_target_pairs={{0,8},{8,0},{4,12},{12,4},{16,24},{24,16},{20,28},{28,20},{1,9},{9... | collective-permute-start | bytes 12582920 | tf_op jit(solution)/shard_map/ppermute | solution.py:17
Sparse Core Ops, SparseCore 0:
  10.4 83.4 all-gather.4
  96.1 79.2 all-gather.6
  177.6 75.2 reduce-scatter.2
  255.1 77.2 reduce-scatter.4
where the time goes:
time: 407 us
  waiting for transfers between devices  295 us (72%)
  matrix products  44.7 us (11%)
  local copies, waits for them, and re-layouts  28.6 us (7%)
  other arithmetic  20.1 us (5%)
  between operations  13.8 us (3%)
  starting transfers between devices  4.09 us (1%)
    ppermute x4, waiting for transfers between devices, from_partner(): return lax.ppermute(block, axis, route)  134 us
    all_gather x2, waiting for transfers between devices, local(): gathered = lax.all_gather(rows_here, 'tensor', axis=0, tiled=True)  131 us
    reduce_scatter x2, waiting for transfers between devices, input_partials(): lax.psum_scatter(rounded, 'tensor', scatter_dimension=0, tiled=True)  30 us
    unnamed x10, local copies, waits for them, and re-layouts  25.5 us
    dot_general x2, matrix products, local(): lax.dot_general(gathered, slope_grad, (((0,), (0,)), ((), ())), preferred...  18.9 us
    broadcast_in_dim x2, other arithmetic, local(): return (weight_now[None], moment_now[None], jnp.stack(grads_out))  17.1 us
    dot_general x2, matrix products, local(): pre = jnp.dot(gathered, weight_now, preferred_element_type=jnp.float32)  13.1 us
    dot_general x2, matrix products, input_partials(): lax.dot_general(slope_grad, weight_now, (((1,), (1,)), ((), ())), preferr...  12.7 us
  transfers between devices with their start and end apart: 8, of which 5 were waited for; matrix products, arithmetic and copies ran while one was open for 19% of the time, Pallas kernels for 0%

commit v1 on v0

v1 whole, which is shorter than its diff:
```python
import functools

import jax
import jax.numpy as jnp
from jax import lax
from jax.experimental import pallas as pl
from jax.experimental.pallas import tpu as pltpu
from jax.sharding import PartitionSpec as P


learn_rate = 0.001
mom_decay = 0.9
first_chunks = 2
last_chunks = 4
tile = 512


def f32(a):
    return a.astype(jnp.float32)


def silu_slope(pre):
    sigma = jax.nn.sigmoid(pre)
    return sigma * (1.0 + pre * (1.0 - sigma))


def slope_body(group, n, place, *refs):
    count = len(group)
    cands, (w_ref, g_ref, x_ref, s_ref, acc) = refs[: 2 * count], refs[2 * count :]
    t = place[0]
    rows = x_ref.shape[0] // count
    i = pl.program_id(0)
    for j, k in enumerate(group):
        part = pl.ds(j * rows, rows)

        @pl.when(t >= k)
        def _():
            x_ref[part, :] = cands[2 * j][...]

        @pl.when(t < k)
        def _():
            x_ref[part, :] = cands[2 * j + 1][...]

    got = jnp.dot(x_ref[...], w_ref[...], preferred_element_type=jnp.float32)

    @pl.when(i == 0)
    def _():
        acc[...] = got

    @pl.when(i > 0)
    def _():
        acc[...] += got

    @pl.when(i == pl.num_programs(0) - 1)
    def _():
        for j, k in enumerate(group):
            part = pl.ds(j * rows, rows)
            shard = lax.rem(t - k + n, n)
            g = f32(g_ref[pl.ds(pl.multiple_of(shard * rows, rows), rows), :])
            s_ref[part, :] = (g * silu_slope(acc[part, :])).astype(jnp.bfloat16)


def slope_step(group, n, place, pairs, weight, grads):
    rows, width = pairs[0][0].shape
    cols = weight.shape[1]
    count = len(group)
    size = min(4 * tile, width)
    flat = [a for pair in pairs for a in pair]
    return pl.pallas_call(
        functools.partial(slope_body, group, n),
        grid_spec=pltpu.PrefetchScalarGridSpec(
            num_scalar_prefetch=1,
            grid=(width // size,),
            in_specs=[pl.BlockSpec((rows, size), lambda i, p: (0, i))] * len(flat)
            + [pl.BlockSpec((size, cols), lambda i, p: (i, 0)), pl.BlockSpec(grads.shape, lambda i, p: (0, 0))],
            out_specs=[
                pl.BlockSpec((count * rows, size), lambda i, p: (0, i)),
                pl.BlockSpec((count * rows, cols), lambda i, p: (0, 0)),
            ],
            scratch_shapes=[pltpu.VMEM((count * rows, cols), jnp.float32)],
        ),
        out_shape=[
            jax.ShapeDtypeStruct((count * rows, width), jnp.bfloat16),
            jax.ShapeDtypeStruct((count * rows, cols), jnp.bfloat16),
        ],
        name="slope_step",
    )(place, *flat, weight, grads)


def partial_body(s_ref, w_ref, *outs):
    value = lax.dot_general(
        s_ref[...], w_ref[...], (((1,), (1,)), ((), ())), preferred_element_type=jnp.float32
    ).astype(jnp.bfloat16)
    rows = outs[0].shape[0]
    for j, out in enumerate(outs):
        out[...] = value[j * rows : (j + 1) * rows]


def partial_step(slope, weight, count):
    width, cols = weight.shape
    rows = slope.shape[0] // count
    size = min(4 * tile, width)
    return pl.pallas_call(
        partial_body,
        grid=(width // size,),
        in_specs=[pl.BlockSpec(slope.shape, lambda i: (0, 0)), pl.BlockSpec((size, cols), lambda i: (i, 0))],
        out_specs=[pl.BlockSpec((rows, size), lambda i: (0, i))] * count,
        out_shape=[jax.ShapeDtypeStruct((rows, width), jnp.bfloat16)] * count,
        name="partial_step",
    )(slope, weight)


def moment_body(count, *refs):
    x = jnp.concatenate([r[...] for r in refs[:count]], axis=0)
    s = jnp.concatenate([r[...] for r in refs[count : 2 * count]], axis=0)
    grad = lax.dot_general(x, s, (((0,), (0,)), ((), ())), preferred_element_type=jnp.float32)
    refs[-1][...] = (mom_decay * f32(refs[-2][...]) + grad).astype(jnp.bfloat16)


def moment_step(blocks, slopes, moment, chunk, chunks):
    width, cols = moment.shape
    size = min(2 * tile, width // chunks // 2)
    steps = width // chunks // size
    first = chunk * steps
    return pl.pallas_call(
        functools.partial(moment_body, len(blocks)),
        grid=(steps,),
        in_specs=[pl.BlockSpec((b.shape[0], size), lambda i: (0, first + i)) for b in blocks]
        + [pl.BlockSpec(s.shape, lambda i: (0, 0)) for s in slopes]
        + [pl.BlockSpec((size, cols), lambda i: (first + i, 0))],
        out_specs=pl.BlockSpec((size, cols), lambda i: (i, 0)),
        out_shape=jax.ShapeDtypeStruct((width // chunks, cols), jnp.bfloat16),
        name="moment_step",
    )(*blocks, *slopes, moment)


def mean_body(half, place, m_ref, mp_ref, w_ref, wp_ref, *refs):
    w_out, m_out, mine = refs[-3:]
    mean = 0.5 * (f32(m_ref[...]) + f32(mp_ref[...]))
    m_out[...] = mean.astype(jnp.bfloat16)
    new = (0.5 * (f32(w_ref[...]) + f32(wp_ref[...])) - learn_rate * mean).astype(jnp.bfloat16)
    w_out[...] = new
    at = pl.program_id(0) - place[1] * half

    @pl.when((at >= 0) & (at < half))
    def _():
        mine[...] = new


def mean_step(place, m, mp, w, wp, chunk, outs):
    rows, cols = m.shape
    size = min(tile, rows // 2)
    steps = rows // size
    half = steps // 2
    first = chunk * steps
    part = pl.BlockSpec((size, cols), lambda i, p: (i, 0))
    whole = pl.BlockSpec((size, cols), lambda i, p: (first + i, 0))
    return pl.pallas_call(
        functools.partial(mean_body, half),
        grid_spec=pltpu.PrefetchScalarGridSpec(
            num_scalar_prefetch=1,
            grid=(steps,),
            in_specs=[part, part, whole, whole] + [pl.BlockSpec(memory_space=pl.ANY)] * len(outs),
            out_specs=[
                whole,
                whole,
                pl.BlockSpec((size, cols), lambda i, p: (jnp.clip(i - p[1] * half, 0, half - 1), 0)),
            ],
        ),
        out_shape=[jax.ShapeDtypeStruct(w.shape, jnp.bfloat16)] * 2
        + [jax.ShapeDtypeStruct((rows // 2, cols), jnp.bfloat16)],
        input_output_aliases={5 + i: i for i in range(len(outs))},
        name="mean_step",
    )(place, m, mp, w, wp, *outs)


def final_body(part, place, m_ref, mp_ref, wa_ref, got_ref, twin_ref, *refs):
    w_out, m_out = refs[-2:]
    mean = 0.5 * (f32(m_ref[...]) + f32(mp_ref[...]))
    m_out[...] = mean.astype(jnp.bfloat16)

    def store(wb):
        w_out[...] = (0.5 * (f32(wa_ref[...]) + f32(wb)) - learn_rate * mean).astype(jnp.bfloat16)

    @pl.when(place[1] == part)
    def _():
        store(got_ref[...])

    @pl.when(place[1] != part)
    def _():
        store(twin_ref[...])


def final_step(place, m, mp, wa, got, twin, chunk, outs):
    rows, cols = m.shape
    size = min(tile, rows)
    steps = rows // size
    first = chunk * steps
    part = pl.BlockSpec((size, cols), lambda i, p: (i, 0))
    whole = pl.BlockSpec((size, cols), lambda i, p: (first + i, 0))
    return pl.pallas_call(
        functools.partial(final_body, chunk % 2),
        grid_spec=pltpu.PrefetchScalarGridSpec(
            num_scalar_prefetch=1,
            grid=(steps,),
            in_specs=[part, part, whole, part, part] + [pl.BlockSpec(memory_space=pl.ANY)] * len(outs),
            out_specs=[whole, whole],
        ),
        out_shape=[jax.ShapeDtypeStruct(wa.shape, jnp.bfloat16)] * 2,
        input_output_aliases={6 + i: i for i in range(len(outs))},
        name="final_step",
    )(place, m, mp, wa, got, twin, *outs)


def xor_route(count, mask):
    return [(r, r ^ mask) for r in range(count) if r ^ mask < count]


def gather(block):
    n = lax.axis_size("tensor")
    ups, downs = [block], [block]
    for k in range(n - 1):
        ups.append(lax.ppermute(ups[-1], "tensor", [(i, i + 1) for i in range(k, n - 1)]))
        downs.append(lax.ppermute(downs[-1], "tensor", [(i, i - 1) for i in range(1, n - k)]))
    return ups, downs


def scatter(parts):
    n = len(parts)
    down_sum = up_sum = None
    for d in range(n - 1, 0, -1):
        a = parts[d] if down_sum is None else (f32(parts[d]) + f32(down_sum)).astype(jnp.bfloat16)
        b = parts[n - d] if up_sum is None else (f32(parts[n - d]) + f32(up_sum)).astype(jnp.bfloat16)
        up_sum = lax.ppermute(b, "tensor", [(i, i + 1) for i in range(n - d)])
        down_sum = lax.ppermute(a, "tensor", [(i, i - 1) for i in range(d, n)])
    total = f32(parts[0])
    if n > 1:
        total = total + f32(down_sum) + f32(up_sum)
    return total.astype(jnp.bfloat16)


def groups_of(n):
    late = sorted({1, n - 1})
    early = [k for k in range(n) if k not in late]
    return [g for g in (early, late) if g]


def slopes_of(place, chains, weight, grads):
    ups, downs = chains
    n = len(ups)
    xs, ss = [], []
    for group in groups_of(n):
        pairs = [(ups[k], downs[n - k] if k else downs[0]) for k in group]
        x, s = slope_step(group, n, place, pairs, weight, grads)
        xs.append(x)
        ss.append(s)
    return xs, ss


def partials_of(slopes, weight, n):
    parts = [None] * n
    groups = groups_of(n)
    for j in reversed(range(len(groups))):
        outs = partial_step(slopes[j], weight, len(groups[j]))
        for k, out in zip(groups[j], outs):
            parts[k] = out
    return parts


def local(weight, momentum, inputs, out_grads):
    replicas = lax.axis_size("replica")
    n = lax.axis_size("tensor")
    r = lax.axis_index("replica")
    place = jnp.stack([lax.axis_index("tensor"), r & 1]).astype(jnp.int32)
    w, m = weight[0], momentum[0]
    twins = xor_route(replicas, 1)
    partners = xor_route(replicas, 2)

    chains = gather(inputs[0])
    wp = lax.ppermute(w, "replica", twins)
    late = max(n - 2, 0)
    following, _, _ = lax.optimization_barrier((inputs[1], chains[0][late], chains[1][late]))
    next_chains = gather(following)

    xs, ss = slopes_of(place, chains, w, out_grads[0])
    moments = []
    for c in range(first_chunks):
        moments.append(moment_step(xs, ss, m, c, first_chunks))
    others = [lax.ppermute(a, "replica", twins) for a in moments]
    first_grad = scatter(partials_of(ss, w, n))
    outs, got, twin = [], [], []
    for c in range(first_chunks):
        *outs, mine = mean_step(place, moments[c], others[c], w, wp, c, outs)
        got.append(lax.ppermute(mine, "replica", partners))
    w, m = outs
    twin = [lax.ppermute(a, "replica", twins) for a in got]

    xs, ss = slopes_of(place, next_chains, w, out_grads[1])
    moments = []
    for c in range(last_chunks):
        moments.append(moment_step(xs, ss, m, c, last_chunks))
    others = [lax.ppermute(a, "replica", partners) for a in moments]
    last_grad = scatter(partials_of(ss, w, n))
    outs = []
    for c in range(last_chunks):
        outs = final_step(place, moments[c], others[c], w, got[c // 2], twin[c // 2], c, outs)
    return (outs[0][None], outs[1][None], jnp.stack([first_grad, last_grad]))


def solution(mesh):
    return jax.shard_map(
        local,
        mesh=mesh,
        in_specs=(
            P("replica", None, "tensor"),
            P("replica", None, "tensor"),
            P(None, ("replica", "tensor"), None),
            P(None, "replica", "tensor"),
        ),
        out_specs=(
            P("replica", None, "tensor"),
            P("replica", None, "tensor"),
            P(None, ("replica", "tensor"), None),
        ),
        check_vma=False,
    )
```

time: 407 us -> 333 us (0.82)
  waiting for transfers between devices: 295 us -> 142 us
  Pallas kernels: 0 us -> 96.6 us
  starting transfers between devices: 4.09 us -> 61.1 us
  matrix products: 44.7 us -> 0 us
  local copies, waits for them, and re-layouts: 28.6 us -> 7.29 us
  between operations: 13.8 us -> 0.96 us
    all_gather x2 -> x0, waiting for transfers between devices: 131 us -> none  [local(): gathered = lax.all_gather(rows_here, 'tensor', axis=0, tiled=True)]
    pallas_call x0 -> x20, Pallas kernels: none -> 96.6 us  [the longest x4 25.4 us: slope_step(): pl.pallas_call(functools.partial(slope_body, group, n), grid_spec=pltpu.P...]
    ppermute x4 -> x35, starting transfers between devices: 3.75 us -> 61.1 us  [the longest x6 21 us: scatter(): up_sum = lax.ppermute(b, 'tensor', [(i, i + 1) for i in range(n - d)])]
    dot_general x6 -> x0, matrix products: 44.7 us -> none  [the longest x2 18.9 us: local(): lax.dot_general(gathered, slope_grad, (((0,), (0,)), ((), ())), preferred...]
    reduce_scatter x2 -> x0, waiting for transfers between devices: 30 us -> none  [input_partials(): lax.psum_scatter(rounded, 'tensor', scatter_dimension=0, tiled=True)]
    unnamed x10 -> x34, local copies, waits for them, and re-layouts: 25.5 us -> 3.36 us
    convert_element_type x0 -> x6, other arithmetic: none -> 17.2 us  [the longest x4 12 us: scatter(): (f32(parts[d]) + f32(down_sum)).astype(jnp.bfloat16)]
    broadcast_in_dim x2 -> x0, other arithmetic: 17.1 us -> none  [local(): return (weight_now[None], moment_now[None], jnp.stack(grads_out))]
  transfers between devices with their start and end apart: 8 -> 35, of which waited for: 5 -> 11; matrix products, arithmetic and copies ran while one was open for 19% -> 7% of each run, Pallas kernels for 0% -> 29%
where the time goes in v1:
time: 333 us; the launch traced here: 331 us
  waiting for transfers between devices  142 us (43%)
  Pallas kernels  96.6 us (29%)
  starting transfers between devices  61.1 us (18%)
  other arithmetic  23 us (7%)
  local copies, waits for them, and re-layouts  7.29 us (2%)
    ppermute x6, waiting for transfers between devices, gather(): lax.ppermute(downs[-1], 'tensor', [(i, i - 1) for i in range(1, n - k)])  79.9 us
    ppermute x4, waiting for transfers between devices, local(): others = [lax.ppermute(a, 'replica', partners) for a in moments]  38.1 us
    pallas_call x4, Pallas kernels, slope_step(): pl.pallas_call(functools.partial(slope_body, group, n), grid_spec=pltpu.P...  25.4 us
    pallas_call x6, Pallas kernels, moment_step(): pl.pallas_call(functools.partial(moment_body, len(blocks)), grid=(steps,)...  21.9 us
    ppermute x6, starting transfers between devices, scatter(): up_sum = lax.ppermute(b, 'tensor', [(i, i + 1) for i in range(n - d)])  21 us
    pallas_call x4, Pallas kernels, final_step(): pl.pallas_call(functools.partial(final_body, chunk % 2), grid_spec=pltpu....  18.3 us
    ppermute x6, starting transfers between devices, gather(): lax.ppermute(ups[-1], 'tensor', [(i, i + 1) for i in range(k, n - 1)])  17.8 us
    pallas_call x4, Pallas kernels, partial_step(): pl.pallas_call(partial_body, grid=(width // size,), in_specs=[pl.BlockSpe...  16.3 us
  transfers between devices with their start and end apart: 35, of which 11 were waited for; matrix products, arithmetic and copies ran while one was open for 7% of the time, Pallas kernels for 29%

profile of v1, /device:TPU:0, one launch (start us, length us, event | category | flops | bytes accessed | tf_op | source)
XLA Modules:
  0.0 331.3 jit_solution(17385728417393852091)
XLA Ops:
  3.6 5.7 %collective-permute-start = (bf16[128,4096]{1,0:T(8,128)(2,1)S(1)}, bf16[128,4096]{1,0:T(8,128)(2,1)S(1)}, u32[]{:S(2)}, u32[]{:S(2)}) collective-permute-start(bf16[128,4096]{1,0:T(8,128)(2,1)S(1)} %get-tuple-element.65.refs_0_.refs_1_), channel_id=1, source_target_pairs={{0,1},{1,2},{2,3},{4,5},{5,6},{6,7},{8,9},{9,10},{10,11},{12,13},{... | collective-permute-start | bytes 3145736 | tf_op jit(solution)/shard_map/ppermute | solution.py:223
  9.3 21.2 %collective-permute-done.2.refs_3_ = bf16[128,4096]{1,0:T(8,128)(2,1)S(1)} collective-permute-done((bf16[128,4096]{1,0:T(8,128)(2,1)S(1)}, bf16[128,4096]{1,0:T(8,128)(2,1)S(1)}, u32[]{:S(2)}, u32[]{:S(2)}) %collective-permute-start.2) | collective-permute-done | bytes 1048608 | tf_op jit(solution)/shard_map/ppermute | solution.py:224
  33.4 23.3 %collective-permute-done.3.refs_3_ = bf16[128,4096]{1,0:T(8,128)(2,1)} collective-permute-done((bf16[128,4096]{1,0:T(8,128)(2,1)S(1)}, bf16[128,4096]{1,0:T(8,128)(2,1)}, u32[]{:S(2)}, u32[]{:S(2)}) %collective-permute-start.3) | collective-permute-done | bytes 1048608 | tf_op jit(solution)/shard_map/ppermute | solution.py:224
  62.6 6.5 %collective-permute-start.4 = (bf16[128,4096]{1,0:T(8,128)(2,1)S(1)}, bf16[128,4096]{1,0:T(8,128)(2,1)}, u32[]{:S(2)}, u32[]{:S(2)}) collective-permute-start(bf16[128,4096]{1,0:T(8,128)(2,1)S(1)} %get-tuple-element.34.refs_0_.refs_1_), channel_id=1, source_target_pairs={{0,1},{1,2},{2,3},{4,5},{5,6},{6,7},{8,9},{9,10},{10,11},{12,13},{... | collective-permute-start | bytes 3145736 | tf_op jit(solution)/shard_map/ppermute | solution.py:223
  70.4 6.4 %slope_step.4 = (bf16[256,4096]{1,0:T(8,128)(2,1)}, bf16[256,512]{1,0:T(8,128)(2,1)}) custom-call(s32[2]{0:T(128)} %pad_add_fusion.place, bf16[128,4096]{1,0:T(8,128)(2,1)} %copy-done.1, bf16[128,4096]{1,0:T(8,128)(2,1)} %copy-done.1, bf16[128,4096]{1,0:T(8,128)(2,1)} %collective-permute-done.1.refs_2_, bf16[128,4096]{1,0:T(8,128)(2,1)} %collective-permute-done.3.refs_3_, ...), custom_call_target="tpu_custom_call" | custom-call | tf_op jit(solution)/shard_map/slope_step/pallas_call | solution.py:69
  76.7 8.2 %collective-permute-done.8.refs_1_ = bf16[128,4096]{1,0:T(8,128)(2,1)} collective-permute-done((bf16[128,4096]{1,0:T(8,128)(2,1)}, bf16[128,4096]{1,0:T(8,128)(2,1)}, u32[]{:S(2)}, u32[]{:S(2)}) %collective-permute-start.8) | collective-permute-done | bytes 1048608 | tf_op jit(solution)/shard_map/ppermute | solution.py:224
  85.0 6.4 %slope_step.5 = (bf16[256,4096]{1,0:T(8,128)(2,1)}, bf16[256,512]{1,0:T(8,128)(2,1)}) custom-call(s32[2]{0:T(128)} %pad_add_fusion.place, bf16[128,4096]{1,0:T(8,128)(2,1)} %copy-done.12, bf16[128,4096]{1,0:T(8,128)(2,1)} %collective-permute-done.8.refs_1_, bf16[128,4096]{1,0:T(8,128)(2,1)} %collective-permute-done.9.refs_2_, bf16[128,4096]{1,0:T(8,128)(2,1)} %copy-done.11, ...), custom_call_target="tpu_custom_call" | custom-call | tf_op jit(solution)/shard_map/slope_step/pallas_call | solution.py:69
  95.7 4.3 %moment_step.6.m_ref = bf16[2048,512]{1,0:T(8,128)(2,1)} custom-call(bf16[256,4096]{1,0:T(8,128)(2,1)} %get-tuple-element.35.refs_0_, bf16[256,4096]{1,0:T(8,128)(2,1)} %get-tuple-element.36.refs_1_, bf16[256,512]{1,0:T(8,128)(2,1)} %get-tuple-element.37.refs_2_.s_ref, bf16[256,512]{1,0:T(8,128)(2,1)} %get-tuple-element.38.refs_3_.s_ref, ...), custom_call_target="tpu_custom_call" | custom-call | tf_op jit(solution)/shard_map/moment_step/pallas_call | solution.py:125
  100.5 4.4 %collective-permute-done.6.refs_3_ = bf16[128,4096]{1,0:T(8,128)(2,1)} collective-permute-done((bf16[128,4096]{1,0:T(8,128)(2,1)S(1)}, bf16[128,4096]{1,0:T(8,128)(2,1)}, u32[]{:S(2)}, u32[]{:S(2)}) %collective-permute-start.6) | collective-permute-done | bytes 1048608 | tf_op jit(solution)/shard_map/ppermute | solution.py:224
  106.9 22.8 %collective-permute-done.7.refs_3_ = bf16[128,4096]{1,0:T(8,128)(2,1)} collective-permute-done((bf16[128,4096]{1,0:T(8,128)(2,1)}, bf16[128,4096]{1,0:T(8,128)(2,1)}, u32[]{:S(2)}, u32[]{:S(2)}) %collective-permute-start.7) | collective-permute-done | bytes 1048608 | tf_op jit(solution)/shard_map/ppermute | solution.py:224
  138.3 6.6 %collective-permute-start.26 = (bf16[128,4096]{1,0:T(8,128)(2,1)}, bf16[128,4096]{1,0:T(8,128)(2,1)}, u32[]{:S(2)}, u32[]{:S(2)}) collective-permute-start(bf16[128,4096]{1,0:T(8,128)(2,1)} %get-tuple-element.58), channel_id=1, source_target_pairs={{0,1},{4,5},{8,9},{12,13},{16,17},{20,21},{24,25},{28,29}} | collective-permute-start | bytes 3145736 | tf_op jit(solution)/shard_map/ppermute | solution.py:234
  149.0 7.4 %mean_step.2 = (bf16[4096,512]{1,0:T(8,128)(2,1)}, bf16[4096,512]{1,0:T(8,128)(2,1)}, bf16[1024,512]{1,0:T(8,128)(2,1)}) custom-call(s32[2]{0:T(128)} %pad_add_fusion.place, bf16[2048,512]{1,0:T(8,128)(2,1)} %moment_step.7.m_ref, bf16[2048,512]{1,0:T(8,128)(2,1)} %collective-permute-done.12.mp_ref, bf16[4096,512]{1,0:T(8,128)(2,1)} %bitcast.4.refs_4_.w_ref, ...), custom_call_target="tpu_custom_call" | custom-call | tf_op jit(solution)/shard_map/mean_step/pallas_call | solution.py:158
  157.6 7.3 %mean_step.3 = (bf16[4096,512]{1,0:T(8,128)(2,1)}, bf16[4096,512]{1,0:T(8,128)(2,1)}, bf16[1024,512]{1,0:T(8,128)(2,1)}) custom-call(s32[2]{0:T(128)} %pad_add_fusion.place, bf16[2048,512]{1,0:T(8,128)(2,1)} %moment_step.6.m_ref, bf16[2048,512]{1,0:T(8,128)(2,1)} %copy-done.6, ...), custom_call_target="tpu_custom_call", output_to_operand_aliasing={{0}: (5, {}), {1}: (6, {})} | custom-call | tf_op jit(solution)/shard_map/mean_step/pallas_call | solution.py:158
  165.0 6.4 %slope_step.7 = (bf16[256,4096]{1,0:T(8,128)(2,1)}, bf16[256,512]{1,0:T(8,128)(2,1)}) custom-call(s32[2]{0:T(128)} %pad_add_fusion.place, bf16[128,4096]{1,0:T(8,128)(2,1)} %collective-permute-done.4.refs_0_, bf16[128,4096]{1,0:T(8,128)(2,1)} %collective-permute-done.13.refs_1_, bf16[128,4096]{1,0:T(8,128)(2,1)} %collective-permute-done.14.refs_2_, ...), custom_call_target="tpu_custom_call" | custom-call | tf_op jit(solution)/shard_map/slope_step/pallas_call | solution.py:69
  185.8 6.4 %slope_step.6 = (bf16[256,4096]{1,0:T(8,128)(2,1)}, bf16[256,512]{1,0:T(8,128)(2,1)}) custom-call(s32[2]{0:T(128)} %pad_add_fusion.place, bf16[128,4096]{1,0:T(8,128)(2,1)} %copy-done, bf16[128,4096]{1,0:T(8,128)(2,1)} %copy-done, bf16[128,4096]{1,0:T(8,128)(2,1)} %copy-done.10, bf16[128,4096]{1,0:T(8,128)(2,1)} %collective-permute-done.7.refs_3_, ...), custom_call_target="tpu_custom_call" | custom-call | tf_op jit(solution)/shard_map/slope_step/pallas_call | solution.py:69
  206.8 12.2 %collective-permute-done.27 = bf16[128,4096]{1,0:T(8,128)(2,1)} collective-permute-done((bf16[128,4096]{1,0:T(8,128)(2,1)}, bf16[128,4096]{1,0:T(8,128)(2,1)}, u32[]{:S(2)}, u32[]{:S(2)}) %collective-permute-start.27) | collective-permute-done | bytes 1048608 | tf_op jit(solution)/shard_map/ppermute | solution.py:234
  219.0 5.4 %collective-permute-start.33 = (bf16[128,4096]{1,0:T(8,128)(2,1)}, bf16[128,4096]{1,0:T(8,128)(2,1)}, u32[]{:S(2)}, u32[]{:S(2)}) collective-permute-start(bf16[128,4096]{1,0:T(8,128)(2,1)} %get-tuple-element.70), channel_id=1, source_target_pairs={{0,1},{1,2},{4,5},{5,6},{8,9},{9,10},{12,13},{13,14},{16,17},{17,1... | collective-permute-start | bytes 3145736 | tf_op jit(solution)/shard_map/ppermute | solution.py:234
  244.6 11.6 %collective-permute-done.20.got_ref = bf16[1024,512]{1,0:T(8,128)(2,1)S(1)} collective-permute-done((bf16[1024,512]{1,0:T(8,128)(2,1)}, bf16[1024,512]{1,0:T(8,128)(2,1)S(1)}, u32[]{:S(2)}, u32[]{:S(2)}) %collective-permute-start.20) | collective-permute-done | bytes 1048608 | tf_op jit(solution)/shard_map/ppermute | solution.py:294
  260.4 15.6 %collective-permute-done.22.mp_ref = bf16[1024,512]{1,0:T(8,128)(2,1)} collective-permute-done((bf16[1024,512]{1,0:T(8,128)(2,1)}, bf16[1024,512]{1,0:T(8,128)(2,1)}, u32[]{:S(2)}, u32[]{:S(2)}) %collective-permute-start.22) | collective-permute-done | bytes 1048608 | tf_op jit(solution)/shard_map/ppermute | solution.py:302
  287.7 4.5 %final_step.4 = (bf16[4096,512]{1,0:T(8,128)(2,1)}, bf16[4096,512]{1,0:T(8,128)(2,1)}) custom-call(s32[2]{0:T(128)} %pad_add_fusion.place, bf16[1024,512]{1,0:T(8,128)(2,1)} %moment_step.11.m_ref, bf16[1024,512]{1,0:T(8,128)(2,1)} %collective-permute-done.22.mp_ref, bf16[4096,512]{1,0:T(8,128)(2,1)} %get-tuple-element.41.refs_4_.wa_ref.w_ref, ...), custom_call_target="tpu_custom_call" | custom-call | tf_op jit(solution)/shard_map/final_step/pallas_call | solution.py:201
  292.2 4.5 %final_step.5 = (bf16[4096,512]{1,0:T(8,128)(2,1)}, bf16[4096,512]{1,0:T(8,128)(2,1)}) custom-call(s32[2]{0:T(128)} %pad_add_fusion.place, bf16[1024,512]{1,0:T(8,128)(2,1)} %moment_step.10.m_ref, bf16[1024,512]{1,0:T(8,128)(2,1)} %collective-permute-done.19.mp_ref, ...), custom_call_target="tpu_custom_call", output_to_operand_aliasing={{0}: (6, {}), {1}: (7, {})} | custom-call | tf_op jit(solution)/shard_map/final_step/pallas_call | solution.py:201
  296.8 21.8 %collective-permute-done.18.mp_ref = bf16[1024,512]{1,0:T(8,128)(2,1)} collective-permute-done((bf16[1024,512]{1,0:T(8,128)(2,1)}, bf16[1024,512]{1,0:T(8,128)(2,1)}, u32[]{:S(2)}, u32[]{:S(2)}) %collective-permute-start.18) | collective-permute-done | bytes 1048608 | tf_op jit(solution)/shard_map/ppermute | solution.py:302
  318.5 4.5 %final_step.6 = (bf16[4096,512]{1,0:T(8,128)(2,1)}, bf16[4096,512]{1,0:T(8,128)(2,1)}) custom-call(s32[2]{0:T(128)} %pad_add_fusion.place, bf16[1024,512]{1,0:T(8,128)(2,1)} %moment_step.9.m_ref, bf16[1024,512]{1,0:T(8,128)(2,1)} %collective-permute-done.18.mp_ref, ...), custom_call_target="tpu_custom_call", output_to_operand_aliasing={{0}: (6, {}), {1}: (7, {})} | custom-call | tf_op jit(solution)/shard_map/final_step/pallas_call | solution.py:201
  323.1 4.7 %final_step.7 = (bf16[4096,512]{1,0:T(8,128)(2,1)}, bf16[4096,512]{1,0:T(8,128)(2,1)}) custom-call(s32[2]{0:T(128)} %pad_add_fusion.place, bf16[1024,512]{1,0:T(8,128)(2,1)} %moment_step.8.m_ref, bf16[1024,512]{1,0:T(8,128)(2,1)} %collective-permute-done.15.mp_ref, ...), custom_call_target="tpu_custom_call", output_to_operand_aliasing={{0}: (6, {}), {1}: (7, {})} | custom-call | tf_op jit(solution)/shard_map/final_step/pallas_call | solution.py:201
  (112 shorter events, 102.5 us)
Async XLA Ops:
  33.4 103.3 %collective-permute-start.11 = (bf16[4096,512]{1,0:T(8,128)(2,1)}, bf16[4096,512]{1,0:T(8,128)(2,1)}, u32[]{:S(2)}, u32[]{:S(2)}) collective-permute-start(bf16[4096,512]{1,0:T(8,128)(2,1)} %bitcast.4.refs_4_.w_ref), channel_id=1, source_target_pairs={{0,4},{4,0},{8,12},{12,8},{16,20},{20,16},{24,28},{28,24},{1,5},{5... | collective-permute-start | bytes 12582920 | tf_op jit(solution)/shard_map/ppermute | solution.py:280
  56.8 28.2 %collective-permute-start.8 = (bf16[128,4096]{1,0:T(8,128)(2,1)}, bf16[128,4096]{1,0:T(8,128)(2,1)}, u32[]{:S(2)}, u32[]{:S(2)}) collective-permute-start(bf16[128,4096]{1,0:T(8,128)(2,1)} %collective-permute-done.3.refs_3_), channel_id=1, source_target_pairs={{1,0},{5,4},{9,8},{13,12},{17,16},{21,20},{25,24},{29,28}} | collective-permute-start | bytes 3145736 | tf_op jit(solution)/shard_map/ppermute | solution.py:224
  62.6 43.6 %collective-permute-start.4 = (bf16[128,4096]{1,0:T(8,128)(2,1)S(1)}, bf16[128,4096]{1,0:T(8,128)(2,1)}, u32[]{:S(2)}, u32[]{:S(2)}) collective-permute-start(bf16[128,4096]{1,0:T(8,128)(2,1)S(1)} %get-tuple-element.34.refs_0_.refs_1_), channel_id=1, source_target_pairs={{0,1},{1,2},{2,3},{4,5},{5,6},{6,7},{8,9},{9,10},{10,11},{12,13},{... | collective-permute-start | bytes 3145736 | tf_op jit(solution)/shard_map/ppermute | solution.py:223
  69.1 35.8 %collective-permute-start.6 = (bf16[128,4096]{1,0:T(8,128)(2,1)S(1)}, bf16[128,4096]{1,0:T(8,128)(2,1)}, u32[]{:S(2)}, u32[]{:S(2)}) collective-permute-start(bf16[128,4096]{1,0:T(8,128)(2,1)S(1)} %get-tuple-element.34.refs_0_.refs_1_), channel_id=1, source_target_pairs={{1,0},{2,1},{3,2},{5,4},{6,5},{7,6},{9,8},{10,9},{11,10},{13,12},{... | collective-permute-start | bytes 3145736 | tf_op jit(solution)/shard_map/ppermute | solution.py:224
  95.7 42.6 %collective-permute-start.12 = (bf16[2048,512]{1,0:T(8,128)(2,1)}, bf16[2048,512]{1,0:T(8,128)(2,1)}, u32[]{:S(2)}, u32[]{:S(2)}) collective-permute-start(bf16[2048,512]{1,0:T(8,128)(2,1)} %moment_step.7.m_ref), channel_id=1, source_target_pairs={{0,4},{4,0},{8,12},{12,8},{16,20},{20,16},{24,28},{28,24},{1,5},{5... | collective-permute-start | bytes 6291464 | tf_op jit(solution)/shard_map/ppermute | solution.py:289
  100.1 56.3 %collective-permute-start.10 = (bf16[2048,512]{1,0:T(8,128)(2,1)}, bf16[2048,512]{1,0:T(8,128)(2,1)S(1)}, u32[]{:S(2)}, u32[]{:S(2)}) collective-permute-start(bf16[2048,512]{1,0:T(8,128)(2,1)} %moment_step.6.m_ref), channel_id=1, source_target_pairs={{0,4},{4,0},{8,12},{12,8},{16,20},{20,16},{24,28},{28,24},{1,5},{5... | collective-permute-start | bytes 6291464 | tf_op jit(solution)/shard_map/ppermute | solution.py:289
  129.7 35.3 %collective-permute-start.13 = (bf16[128,4096]{1,0:T(8,128)(2,1)}, bf16[128,4096]{1,0:T(8,128)(2,1)}, u32[]{:S(2)}, u32[]{:S(2)}) collective-permute-start(bf16[128,4096]{1,0:T(8,128)(2,1)} %collective-permute-done.7.refs_3_), channel_id=1, source_target_pairs={{1,0},{5,4},{9,8},{13,12},{17,16},{21,20},{25,24},{29,28}} | collective-permute-start | bytes 3145736 | tf_op jit(solution)/shard_map/ppermute | solution.py:224
  131.0 34.0 %collective-permute-start.14 = (bf16[128,4096]{1,0:T(8,128)(2,1)S(1)}, bf16[128,4096]{1,0:T(8,128)(2,1)}, u32[]{:S(2)}, u32[]{:S(2)}) collective-permute-start(bf16[128,4096]{1,0:T(8,128)(2,1)S(1)} %collective-permute-done.5.refs_2_), channel_id=1, source_target_pairs={{2,3},{6,7},{10,11},{14,15},{18,19},{22,23},{26,27},{30,31}} | collective-permute-start | bytes 3145736 | tf_op jit(solution)/shard_map/ppermute | solution.py:223
  136.7 40.9 %collective-permute-start.23 = (bf16[128,4096]{1,0:T(8,128)(2,1)}, bf16[128,4096]{1,0:T(8,128)(2,1)}, u32[]{:S(2)}, u32[]{:S(2)}) collective-permute-start(bf16[128,4096]{1,0:T(8,128)(2,1)} %get-tuple-element.60), channel_id=1, source_target_pairs={{3,2},{7,6},{11,10},{15,14},{19,18},{23,22},{27,26},{31,30}} | collective-permute-start | bytes 3145736 | tf_op jit(solution)/shard_map/ppermute | solution.py:235
  138.3 39.3 %collective-permute-start.26 = (bf16[128,4096]{1,0:T(8,128)(2,1)}, bf16[128,4096]{1,0:T(8,128)(2,1)}, u32[]{:S(2)}, u32[]{:S(2)}) collective-permute-start(bf16[128,4096]{1,0:T(8,128)(2,1)} %get-tuple-element.58), channel_id=1, source_target_pairs={{0,1},{4,5},{8,9},{12,13},{16,17},{20,21},{24,25},{28,29}} | collective-permute-start | bytes 3145736 | tf_op jit(solution)/shard_map/ppermute | solution.py:234
  181.1 37.9 %collective-permute-start.27 = (bf16[128,4096]{1,0:T(8,128)(2,1)}, bf16[128,4096]{1,0:T(8,128)(2,1)}, u32[]{:S(2)}, u32[]{:S(2)}) collective-permute-start(bf16[128,4096]{1,0:T(8,128)(2,1)} %get-tuple-element.68), channel_id=1, source_target_pairs={{0,1},{1,2},{4,5},{5,6},{8,9},{9,10},{12,13},{13,14},{16,17},{17,1... | collective-permute-start | bytes 3145736 | tf_op jit(solution)/shard_map/ppermute | solution.py:234
  183.4 46.7 %collective-permute-start.24 = (bf16[128,4096]{1,0:T(8,128)(2,1)}, bf16[128,4096]{1,0:T(8,128)(2,1)}, u32[]{:S(2)}, u32[]{:S(2)}) collective-permute-start(bf16[128,4096]{1,0:T(8,128)(2,1)} %get-tuple-element.67), channel_id=1, source_target_pairs={{2,1},{3,2},{6,5},{7,6},{10,9},{11,10},{14,13},{15,14},{18,17},{19... | collective-permute-start | bytes 3145736 | tf_op jit(solution)/shard_map/ppermute | solution.py:235
  185.0 45.9 %collective-permute-start.16 = (bf16[1024,512]{1,0:T(8,128)(2,1)}, bf16[1024,512]{1,0:T(8,128)(2,1)S(1)}, u32[]{:S(2)}, u32[]{:S(2)}) collective-permute-start(bf16[1024,512]{1,0:T(8,128)(2,1)} %get-tuple-element.47), channel_id=1, source_target_pairs={{0,8},{4,12},{8,0},{12,4},{16,24},{20,28},{24,16},{28,20},{1,9},{5... | collective-permute-start | bytes 3145736 | tf_op jit(solution)/shard_map/ppermute | solution.py:294
  199.6 34.2 %collective-permute-start.19 = (bf16[1024,512]{1,0:T(8,128)(2,1)}, bf16[1024,512]{1,0:T(8,128)(2,1)}, u32[]{:S(2)}, u32[]{:S(2)}) collective-permute-start(bf16[1024,512]{1,0:T(8,128)(2,1)} %moment_step.10.m_ref), channel_id=1, source_target_pairs={{0,8},{4,12},{8,0},{12,4},{16,24},{20,28},{24,16},{28,20},{1,9},{5... | collective-permute-start | bytes 3145736 | tf_op jit(solution)/shard_map/ppermute | solution.py:302
  202.4 53.8 %collective-permute-start.20 = (bf16[1024,512]{1,0:T(8,128)(2,1)}, bf16[1024,512]{1,0:T(8,128)(2,1)S(1)}, u32[]{:S(2)}, u32[]{:S(2)}) collective-permute-start(bf16[1024,512]{1,0:T(8,128)(2,1)} %get-tuple-element.48), channel_id=1, source_target_pairs={{0,8},{4,12},{8,0},{12,4},{16,24},{20,28},{24,16},{28,20},{1,9},{5... | collective-permute-start | bytes 3145736 | tf_op jit(solution)/shard_map/ppermute | solution.py:294
  219.0 38.5 %collective-permute-start.33 = (bf16[128,4096]{1,0:T(8,128)(2,1)}, bf16[128,4096]{1,0:T(8,128)(2,1)}, u32[]{:S(2)}, u32[]{:S(2)}) collective-permute-start(bf16[128,4096]{1,0:T(8,128)(2,1)} %get-tuple-element.70), channel_id=1, source_target_pairs={{0,1},{1,2},{4,5},{5,6},{8,9},{9,10},{12,13},{13,14},{16,17},{17,1... | collective-permute-start | bytes 3145736 | tf_op jit(solution)/shard_map/ppermute | solution.py:234
  230.1 45.9 %collective-permute-start.22 = (bf16[1024,512]{1,0:T(8,128)(2,1)}, bf16[1024,512]{1,0:T(8,128)(2,1)}, u32[]{:S(2)}, u32[]{:S(2)}) collective-permute-start(bf16[1024,512]{1,0:T(8,128)(2,1)} %moment_step.11.m_ref), channel_id=1, source_target_pairs={{0,8},{4,12},{8,0},{12,4},{16,24},{20,28},{24,16},{28,20},{1,9},{5... | collective-permute-start | bytes 3145736 | tf_op jit(solution)/shard_map/ppermute | solution.py:302
  230.9 45.8 %collective-permute-start.28 = (bf16[128,4096]{1,0:T(8,128)(2,1)}, bf16[128,4096]{1,0:T(8,128)(2,1)}, u32[]{:S(2)}, u32[]{:S(2)}) collective-permute-start(bf16[128,4096]{1,0:T(8,128)(2,1)} %add_convert_fusion.4), channel_id=1, source_target_pairs={{0,1},{1,2},{2,3},{4,5},{5,6},{6,7},{8,9},{9,10},{10,11},{12,13},{... | collective-permute-start | bytes 3145736 | tf_op jit(solution)/shard_map/ppermute | solution.py:234
  233.8 44.2 %collective-permute-start.30 = (bf16[128,4096]{1,0:T(8,128)(2,1)}, bf16[128,4096]{1,0:T(8,128)(2,1)}, u32[]{:S(2)}, u32[]{:S(2)}) collective-permute-start(bf16[128,4096]{1,0:T(8,128)(2,1)} %get-tuple-element.69), channel_id=1, source_target_pairs={{2,1},{3,2},{6,5},{7,6},{10,9},{11,10},{14,13},{15,14},{18,17},{19... | collective-permute-start | bytes 3145736 | tf_op jit(solution)/shard_map/ppermute | solution.py:235
  276.0 47.1 %collective-permute-start.15 = (bf16[1024,512]{1,0:T(8,128)(2,1)S(1)}, bf16[1024,512]{1,0:T(8,128)(2,1)}, u32[]{:S(2)}, u32[]{:S(2)}) collective-permute-start(bf16[1024,512]{1,0:T(8,128)(2,1)S(1)} %copy-done.4), channel_id=1, source_target_pairs={{0,8},{4,12},{8,0},{12,4},{16,24},{20,28},{24,16},{28,20},{1,9},{5... | collective-permute-start | bytes 3145736 | tf_op jit(solution)/shard_map/ppermute | solution.py:302
  276.8 41.8 %collective-permute-start.18 = (bf16[1024,512]{1,0:T(8,128)(2,1)}, bf16[1024,512]{1,0:T(8,128)(2,1)}, u32[]{:S(2)}, u32[]{:S(2)}) collective-permute-start(bf16[1024,512]{1,0:T(8,128)(2,1)} %moment_step.9.m_ref), channel_id=1, source_target_pairs={{0,8},{4,12},{8,0},{12,4},{16,24},{20,28},{24,16},{28,20},{1,9},{5... | collective-permute-start | bytes 3145736 | tf_op jit(solution)/shard_map/ppermute | solution.py:302
  278.0 40.5 %collective-permute-start.17 = (bf16[1024,512]{1,0:T(8,128)(2,1)S(1)}, bf16[1024,512]{1,0:T(8,128)(2,1)}, u32[]{:S(2)}, u32[]{:S(2)}) collective-permute-start(bf16[1024,512]{1,0:T(8,128)(2,1)S(1)} %collective-permute-done.16.got_ref), channel_id=1, source_target_pairs={{0,4},{4,0},{8,12},{12,8},{16,20},{20,16},{24,28},{28,24},{1,5},{5... | collective-permute-start | bytes 3145736 | tf_op jit(solution)/shard_map/ppermute | solution.py:296
  280.5 47.3 %collective-permute-start.34 = (bf16[128,4096]{1,0:T(8,128)(2,1)}, bf16[128,4096]{1,0:T(8,128)(2,1)}, u32[]{:S(2)}, u32[]{:S(2)}) collective-permute-start(bf16[128,4096]{1,0:T(8,128)(2,1)} %add_convert_fusion.1), channel_id=1, source_target_pairs={{0,1},{1,2},{2,3},{4,5},{5,6},{6,7},{8,9},{9,10},{10,11},{12,13},{... | collective-permute-start | bytes 3145736 | tf_op jit(solution)/shard_map/ppermute | solution.py:234
  284.7 43.1 %collective-permute-start.31 = (bf16[128,4096]{1,0:T(8,128)(2,1)}, bf16[128,4096]{1,0:T(8,128)(2,1)}, u32[]{:S(2)}, u32[]{:S(2)}) collective-permute-start(bf16[128,4096]{1,0:T(8,128)(2,1)} %add_convert_fusion.2), channel_id=1, source_target_pairs={{1,0},{2,1},{3,2},{5,4},{6,5},{7,6},{9,8},{10,9},{11,10},{13,12},{... | collective-permute-start | bytes 3145736 | tf_op jit(solution)/shard_map/ppermute | solution.py:235
  (28 other events, 710.3 us)
